TPU v7x, 128 devices: a whole 4x4x4 slice. The times are simulated.
128 devices in a mesh: group: 8 (over y, core), dev: 16 (over z, x).
Axes of the slice: x: 4, y: 4, z: 4, core: 2. Of those that a mesh axis runs over, the one named last changes fastest.
Arguments:
- primary_q: bfloat16 [256, 3584, 1024], P(('group', 'dev')), may hold values from -0.09375 to 0.09375
- primary_scales: bfloat16 [256, 28, 8], P(('group', 'dev')), may hold values from 0.5 to 2
- new_place: int32 [128], P(('group', 'dev')), may hold values from 0 to 255, as said below
- tokens: bfloat16 [2048, 3584], P(('group', 'dev')), may hold values from -6 to 6
- experts: int32 [2048, 8], P(('group', 'dev')), may hold values from 0 to 255, all different within a row
- replica: int32 [2048, 8], P(('group', 'dev')), may hold values from 0 to 1
- route_num: int32 [2048, 8], P(('group', 'dev')), may hold values from 1 to 16
Outputs:
- new_weights: bfloat16 [128, 3584, 1024], P(('group', 'dev'))
- new_scales: bfloat16 [128, 28, 8], P(('group', 'dev'))
- hidden_out: bfloat16 [2048, 8, 1024], P(('group', 'dev'))
- slot_load: int32 [128, 3], P(('group', 'dev'))
Inputs may be any that keep to these rules, and one draw needn't show every extreme that they name: `new_place`: the redundant slots of the 16 devices of one group hold 16 different experts, each with its primary copy on a device of that group.
All inputs are finite; a program needn't handle non-finite values.
Results may differ from a plain program's by a relative error of at most 0.0057.
Values may be sent and summed in bfloat16 or wider, within the bound.
A program may use at most 192 MiB of HBM per device.

v0:
```python
import jax
import jax.numpy as jnp
from jax import lax
from jax.sharding import PartitionSpec as P

D = 3584
FF = 1024
TILE = 128
CAP = 2


def dequantize(values, scales):
    tile_grid = values.astype(jnp.float32).reshape(D // TILE, TILE, FF // TILE, TILE)
    scaled = tile_grid * scales.astype(jnp.float32)[:, None, :, None]
    return scaled.reshape(D, FF).astype(jnp.bfloat16)


def spread_parts(values, scales, parts_count):
    holding, width_in, hidden = values.shape
    split_values = values.reshape(holding, parts_count, width_in // parts_count, hidden)
    split_scales = jnp.broadcast_to(scales[:, None], (holding, parts_count) + scales.shape[1:])
    return (split_values, split_scales)


def pick_parts(got_values, got_scales, wanted, first_dev):
    holding = got_values.shape[0]
    parts_count = got_values.shape[1]
    chosen = wanted % holding * parts_count + (wanted // holding - first_dev)
    values = got_values.reshape((holding * parts_count,) + got_values.shape[2:])[chosen]
    scales = got_scales.reshape((holding * parts_count,) + got_scales.shape[2:])[chosen]
    return (values, scales)


def per_device(primary_q, primary_scales, new_place, tokens, experts, replica, route_num):
    place_all = lax.all_gather(new_place, ("group", "dev"), axis=0, tiled=True)
    holding = primary_q.shape[0]
    parts_count = lax.axis_size("dev")
    first_dev = lax.axis_index("group") * parts_count
    wanted = lax.dynamic_slice_in_dim(place_all, first_dev, parts_count)
    split_values, split_scales = spread_parts(primary_q, primary_scales, parts_count)
    got_values, got_scales = (
        lax.all_to_all(split_values, "dev", split_axis=1, concat_axis=1, tiled=True),
        lax.all_to_all(split_scales, "dev", split_axis=1, concat_axis=1, tiled=True),
    )
    send_values, send_scales = pick_parts(got_values, got_scales, wanted, first_dev)
    back_values, back_scales = (
        lax.all_to_all(send_values, "dev", split_axis=0, concat_axis=0, tiled=True),
        lax.all_to_all(send_scales, "dev", split_axis=0, concat_axis=0, tiled=True),
    )
    new_weights = back_values.reshape((1, D, FF))
    new_scales = back_scales[0:1]
    row_count, top_count = experts.shape
    pair_count = row_count * top_count
    device_count = place_all.shape[0]
    expert_flat = experts.reshape(pair_count)
    device_ids = jnp.arange(device_count, dtype=jnp.int32)
    matched = expert_flat[:, None] == place_all[None, :]
    has_copy = jnp.any(matched, axis=1)
    holder = jnp.sum(jnp.where(matched, device_ids[None, :], 0), axis=1)
    use_copy = (replica.reshape(pair_count) == 1) & has_copy
    target = jnp.where(use_copy, holder, expert_flat // holding)
    slot_id = jnp.where(use_copy, holding, expert_flat % holding)
    pair_order = jnp.arange(pair_count)
    earlier = (target[:, None] == target[None, :]) & (pair_order[None, :] < pair_order[:, None])
    position = jnp.sum(earlier, axis=1)
    served = position < CAP
    cell_count = device_count * CAP
    cell_index = target * CAP + position
    placed = (cell_index[None, :] == jnp.arange(cell_count)[:, None]) & served[None, :]
    row_hits = jnp.any(placed.reshape(cell_count, row_count, top_count), axis=2)
    row_buffer = jnp.dot(row_hits.astype(jnp.bfloat16), tokens, preferred_element_type=jnp.float32)
    row_buffer = row_buffer.astype(jnp.bfloat16).reshape(device_count, CAP, D)
    code_values = jnp.sum(jnp.where(placed, slot_id[None, :] + 1, 0), axis=1) - 1
    code_buffer = code_values.astype(jnp.float32).astype(jnp.bfloat16).reshape(device_count, CAP)
    matrices = [dequantize(primary_q[member], primary_scales[member]) for member in range(holding)]
    matrices.append(dequantize(new_weights[0], new_scales[0]))
    joined = jnp.concatenate(matrices, axis=1)
    row_block = lax.all_to_all(
        row_buffer, ("group", "dev"), split_axis=0, concat_axis=0, tiled=True
    )
    slot_codes = lax.all_to_all(
        code_buffer, ("group", "dev"), split_axis=0, concat_axis=0, tiled=True
    )
    leading, item_count, width_in = row_block.shape
    product = jnp.dot(
        row_block.reshape(leading * item_count, width_in),
        joined,
        preferred_element_type=jnp.float32,
    )
    flat_codes = slot_codes.reshape(leading * item_count).astype(jnp.float32)
    picked = jnp.zeros((leading * item_count, FF), jnp.float32)
    tallies = []
    for member in range(holding + 1):
        chosen = flat_codes == member
        picked = picked + jnp.where(
            chosen[:, None], product[:, member * FF : (member + 1) * FF], 0.0
        )
        tallies.append(chosen.astype(jnp.float32))
    activated = jax.nn.silu(picked).astype(jnp.bfloat16).reshape(leading, item_count, FF)
    activated, tallies = (
        activated,
        jnp.stack(tallies, axis=1).reshape(leading, item_count, holding + 1),
    )
    returned = lax.all_to_all(activated, ("group", "dev"), split_axis=0, concat_axis=0, tiled=True)
    dest_hit = (target[None, :] == device_ids[:, None]) & served[None, :]
    slot_hit = slot_id[:, None] == jnp.arange(holding + 1)[None, :]
    counted = jnp.dot(
        dest_hit.astype(jnp.float32), slot_hit.astype(jnp.float32), precision=lax.Precision.HIGHEST
    )
    summed = lax.psum_scatter(counted, ("group", "dev"), scatter_dimension=0, tiled=True)
    slot_load = summed.astype(jnp.int32)
    selected = jnp.dot(
        placed.T.astype(jnp.bfloat16),
        returned.reshape(cell_count, FF),
        preferred_element_type=jnp.float32,
    )
    weight = route_num.reshape(pair_count).astype(jnp.float32) / 16.0
    hidden_out = (selected * weight[:, None]).astype(jnp.bfloat16).reshape(row_count, top_count, FF)
    return (new_weights, new_scales, hidden_out, slot_load)


def solution(mesh):
    in_specs = (
        P(("group", "dev"), None, None),
        P(("group", "dev"), None, None),
        P(("group", "dev")),
        P(("group", "dev"), None),
        P(("group", "dev"), None),
        P(("group", "dev"), None),
        P(("group", "dev"), None),
    )
    out_specs = (
        P(("group", "dev"), None, None),
        P(("group", "dev"), None, None),
        P(("group", "dev"), None, None),
        P(("group", "dev"), None),
    )
    return jax.shard_map(
        per_device, mesh=mesh, in_specs=in_specs, out_specs=out_specs, check_vma=False
    )
```

profile of v0, /device:TPU:1, one launch (start us, length us, event | category | flops | bytes accessed | tf_op | source)
XLA Modules:
  0.0 594.2 jit_solution(13034104524677342891)
XLA Ops:
  0.6 0.0 copy-start
  0.6 0.7 broadcast_bitcast_fusion
  1.4 0.7 reshape.356
  2.1 8.4 %all-to-all-start.2 = ((bf16[16,2,224]{2,1,0:T(2,128)(2,1)}), bf16[16,2,224]{2,1,0:T(2,128)(2,1)S(1)}, u32[]{:S(2)}, u32[]{:S(2)}) async-start(bf16[16,2,224]{2,1,0:T(2,128)(2,1)} %reshape.356), calls=%async_computation.2 | async-start | bytes 32768 | tf_op jit(solution)/shard_map/all_to_all | solution.py:43
  11.2 0.1 dynamic-update-slice
  11.3 66.6 %all-reduce = s32[128]{0:T(128)S(1)} all-reduce(s32[128]{0:T(128)S(1)} %dynamic-update-slice), channel_id=1, replica_groups=mesh['group'=8,'dev'=16] {'group','dev'}, use_global_device_ids=true, to_apply=%add | all-reduce | flops 128 | bytes 1024
  77.9 0.8 copy.62
  78.6 0.1 eq.145
  78.7 0.2 compare_reduce_fusion.3
  78.9 0.2 fusion.17
  79.1 0.8 copy.61
  79.9 0.1 eq.144
  80.0 0.2 convert_reduce_fusion
  80.2 0.1 select_reduce_fusion
  80.3 0.1 compare_select_fusion.1
  80.4 0.8 convert_element_type.161
  81.2 0.0 all-to-all-done.2
  81.2 4.9 all-to-all-start.4
  86.1 0.1 reshape.357
  86.3 1.2 gather_fusion.1
  87.4 8.4 %all-to-all-done.4 = bf16[128,1,2]{2,1,0:T(2,128)(2,1)S(1)} async-done(((bf16[128,1,2]{2,1,0:T(2,128)(2,1)}), bf16[128,1,2]{2,1,0:T(2,128)(2,1)S(1)}, u32[]{:S(2)}, u32[]{:S(2)}) %all-to-all-start.4) | async-done | bytes 544 | tf_op jit(solution)/shard_map/all_to_all | solution.py:81
  95.8 3.5 all-to-all-start.3
  99.3 13.7 %copy.58 = bf16[2,16,224,1024]{3,2,0,1:T(8,128)(2,1)} copy(bf16[2,16,224,1024]{3,2,1,0:T(8,128)(2,1)} %bitcast.49) | data formatting | bytes 29360128 | tf_op jit(solution)/shard_map/reshape | solution.py:20
  113.0 6.6 %all-to-all-start = ((bf16[2,16,224,1024]{3,2,0,1:T(8,128)(2,1)}), bf16[2,16,224,1024]{3,2,0,1:T(8,128)(2,1)}, u32[]{:S(2)}, u32[]{:S(2)}) async-start(bf16[2,16,224,1024]{3,2,0,1:T(8,128)(2,1)} %copy.58), calls=%async_computation | async-start | bytes 29360128 | tf_op jit(solution)/shard_map/all_to_all | solution.py:42
  119.7 0.1 reduce_sum.35
  119.8 0.1 reduce_sum.34
  119.8 0.1 reduce_or.21
  120.0 0.1 fusion.16
  120.1 0.7 convolution_convert_fusion
  120.8 1.7 reshape.322
  122.5 212.4 %all-to-all-done = bf16[2,16,224,1024]{3,2,0,1:T(8,128)(2,1)} async-done(((bf16[2,16,224,1024]{3,2,0,1:T(8,128)(2,1)}), bf16[2,16,224,1024]{3,2,0,1:T(8,128)(2,1)}, u32[]{:S(2)}, u32[]{:S(2)}) %all-to-all-start) | async-done | bytes 14680096 | tf_op jit(solution)/shard_map/all_to_all | solution.py:42
  334.9 7.7 %all-to-all-start.5 = ((bf16[128,2,3584]{2,1,0:T(2,128)(2,1)}), bf16[128,2,3584]{2,1,0:T(2,128)(2,1)S(1)}, u32[]{:S(2)}, u32[]{:S(2)}) async-start(bf16[128,2,3584]{2,1,0:T(2,128)(2,1)} %reshape.322), calls=%async_computation.5 | async-start | bytes 3670016 | tf_op jit(solution)/shard_map/all_to_all | solution.py:78
  342.5 13.7 %copy.59 = bf16[2,16,224,1024]{3,2,1,0:T(8,128)(2,1)} copy(bf16[2,16,224,1024]{3,2,0,1:T(8,128)(2,1)} %all-to-all-done) | data formatting | bytes 29360128 | tf_op jit(solution)/shard_map/all_to_all | solution.py:42
  356.2 9.2 %gather_fusion = bf16[16,224,1024]{2,1,0:T(8,128)(2,1)} fusion(bf16[32,224,1024]{2,1,0:T(8,128)(2,1)} %bitcast.53, s32[1024]{0:T(1024)S(1)} %pad_clamp_fusion), kind=kCustom, calls=%fused_computation | custom fusion | bytes 14680128 | tf_op jit(solution)/shard_map/gather | solution.py:29
  365.5 3.9 all-to-all-done.5
  369.4 4.9 all-to-all-start.1
  374.3 0.1 copy.68
  374.4 0.1 copy.69
  374.5 1.0 mul.65
  375.5 6.2 %mul.68 = f32[28,128,8,128]{3,2,1,0:T(8,128)} broadcast(f32[28,8]{1,0:T(8,128)S(1)} %copy.69), dimensions={0,2} | broadcast | bytes 14680960 | tf_op jit(solution)/shard_map/mul | solution.py:14
  381.7 18.6 %fusion.8 = (bf16[3584,1024]{1,0:T(8,128)(2,1)}, bf16[3584,1024]{1,0:T(8,128)(2,1)}) fusion(f32[448,8,8,128]{3,2,1,0:T(8,128)S(1)} %bitcast.50, bf16[2,3584,1024]{2,1,0:T(8,128)(2,1)} %param.7, f32[448,8,8,128]{3,2,1,0:T(8,128)} %bitcast.51), kind=kLoop, calls=%fused_computation.13 | loop fusion | flops 22020096 | bytes 58720256 | tf_op jit(solution)/shard_map/convert_element_type | solution.py:15
  400.3 0.6 compare_reduce_fusion.2
  401.0 0.1 eq.167
  401.1 0.1 eq.164
  401.3 0.1 eq.158
  401.4 0.6 bitcast_convert_fusion
  402.0 0.1 copy.70
  402.1 1.7 reshape.323
  403.8 77.2 %all-to-all-done.1 = bf16[16,224,1024]{2,1,0:T(8,128)(2,1)} async-done(((bf16[16,224,1024]{2,1,0:T(8,128)(2,1)}), bf16[16,224,1024]{2,1,0:T(8,128)(2,1)}, u32[]{:S(2)}, u32[]{:S(2)}) %all-to-all-start.1) | async-done | bytes 7340064 | tf_op jit(solution)/shard_map/all_to_all | solution.py:47
  480.9 1.0 mul.71
  482.0 9.2 %fusion.6 = bf16[3584,1024]{1,0:T(8,128)(2,1)} fusion(f32[448,8,8,128]{3,2,1,0:T(8,128)S(1)} %bitcast.52, bf16[16,224,1024]{2,1,0:T(8,128)(2,1)} %all-to-all-done.1), kind=kLoop, calls=%fused_computation.9 | loop fusion | flops 11010048 | bytes 29360128 | tf_op jit(solution)/shard_map/convert_element_type | solution.py:15
  491.2 0.0 copy-start.4
  491.2 15.5 %fusion = f32[256,3072]{1,0:T(8,128)S(1)} fusion(bf16[256,3584]{1,0:T(8,128)(2,1)S(1)} %copy-done.2, bf16[3584,1024]{1,0:T(8,128)(2,1)} %fusion.6, bf16[3584,1024]{1,0:T(8,128)(2,1)} %get-tuple-element.12, bf16[3584,1024]{1,0:T(8,128)(2,1)S(1)} %bitcast.55), kind=kOutput, calls=%fused_computation.2 | convolution fusion | flops 5703204864 | bytes 27000832 | tf_op jit(solution)/shard_map/dot_general | solution.py:85
  506.8 0.5 multiply_convert_fusion
  507.2 1.0 reshape.324
  508.2 9.2 %all-to-all-start.6 = ((bf16[128,2,1024]{2,1,0:T(2,128)(2,1)}), bf16[128,2,1024]{2,1,0:T(2,128)(2,1)S(1)}, u32[]{:S(2)}, u32[]{:S(2)}) async-start(bf16[128,2,1024]{2,1,0:T(2,128)(2,1)} %reshape.324), calls=%async_computation.6 | async-start | bytes 1048576 | tf_op jit(solution)/shard_map/all_to_all | solution.py:104
  517.5 0.1 copy.71
  517.5 0.1 div.50
  517.6 0.2 fusion.21
  517.8 67.6 %all-reduce.1 = f32[128,3]{1,0:T(8,128)S(1)} all-reduce(f32[128,3]{1,0:T(8,128)S(1)} %fusion.21), channel_id=2, replica_groups=mesh['group'=8,'dev'=16] {'group','dev'}, use_global_device_ids=true, to_apply=%region_5.6.clone | all-reduce | flops 384 | bytes 3072
  585.4 0.5 dynamic-slice_convert_fusion
  586.0 0.2 reshape.325
  586.2 1.0 fusion.10
  587.1 7.0 %copy.81 = bf16[1,3584,1024]{2,1,0:T(8,128)(2,1)} copy(bf16[1,3584,1024]{2,1,0:T(8,128)(2,1)} %bitcast.2) | data formatting | bytes 14680064
  (27 shorter events, 0.1 us)
Async XLA Ops:
  0.6 119.5 %copy-start = (bf16[16,3584]{1,0:T(8,128)(2,1)S(1)}, bf16[16,3584]{1,0:T(8,128)(2,1)}, u32[]{:S(2)}) copy-start(bf16[16,3584]{1,0:T(8,128)(2,1)} %param.10) | copy-start | bytes 344068
  2.1 79.1 %all-to-all-start.2 = ((bf16[16,2,224]{2,1,0:T(2,128)(2,1)}), bf16[16,2,224]{2,1,0:T(2,128)(2,1)S(1)}, u32[]{:S(2)}, u32[]{:S(2)}) async-start(bf16[16,2,224]{2,1,0:T(2,128)(2,1)} %reshape.356), calls=%async_computation.2 | async-start | bytes 32768 | tf_op jit(solution)/shard_map/all_to_all | solution.py:43
  81.2 14.6 %all-to-all-start.4 = ((bf16[128,1,2]{2,1,0:T(2,128)(2,1)}), bf16[128,1,2]{2,1,0:T(2,128)(2,1)S(1)}, u32[]{:S(2)}, u32[]{:S(2)}) async-start(bf16[128,1,2]{2,1,0:T(2,128)(2,1)} %convert_element_type.161), calls=%async_computation.4 | async-start | bytes 131072 | tf_op jit(solution)/shard_map/all_to_all | solution.py:81
  95.8 17.2 %all-to-all-start.3 = ((bf16[16,28,8]{1,2,0:T(8,128)(2,1)}), bf16[16,28,8]{1,2,0:T(8,128)(2,1)S(1)}, u32[]{:S(2)}, u32[]{:S(2)}) async-start(bf16[16,28,8]{1,2,0:T(8,128)(2,1)} %gather_fusion.1), calls=%async_computation.3 | async-start | bytes 65536 | tf_op jit(solution)/shard_map/all_to_all | solution.py:48
  113.0 221.8 %all-to-all-start = ((bf16[2,16,224,1024]{3,2,0,1:T(8,128)(2,1)}), bf16[2,16,224,1024]{3,2,0,1:T(8,128)(2,1)}, u32[]{:S(2)}, u32[]{:S(2)}) async-start(bf16[2,16,224,1024]{3,2,0,1:T(8,128)(2,1)} %copy.58), calls=%async_computation | async-start | bytes 29360128 | tf_op jit(solution)/shard_map/all_to_all | solution.py:42
  334.9 34.5 %all-to-all-start.5 = ((bf16[128,2,3584]{2,1,0:T(2,128)(2,1)}), bf16[128,2,3584]{2,1,0:T(2,128)(2,1)S(1)}, u32[]{:S(2)}, u32[]{:S(2)}) async-start(bf16[128,2,3584]{2,1,0:T(2,128)(2,1)} %reshape.322), calls=%async_computation.5 | async-start | bytes 3670016 | tf_op jit(solution)/shard_map/all_to_all | solution.py:78
  365.5 8.8 %copy-start.3 = (bf16[2,28,8]{1,2,0:T(8,128)(2,1)S(1)}, bf16[2,28,8]{1,2,0:T(8,128)(2,1)}, u32[]{:S(2)}) copy-start(bf16[2,28,8]{1,2,0:T(8,128)(2,1)} %param.8) | copy-start | bytes 2692
  369.4 111.5 %all-to-all-start.1 = ((bf16[16,224,1024]{2,1,0:T(8,128)(2,1)}), bf16[16,224,1024]{2,1,0:T(8,128)(2,1)}, u32[]{:S(2)}, u32[]{:S(2)}) async-start(bf16[16,224,1024]{2,1,0:T(8,128)(2,1)} %gather_fusion), calls=%async_computation.1 | async-start | bytes 14680064 | tf_op jit(solution)/shard_map/all_to_all | solution.py:47
  480.9 10.3 %slice-start = ((s8[7340032]{0:T(1024)(128)(4,1)}), s8[4194304]{0:T(1024)(128)(4,1)S(1)}, s32[]{:S(2)}) async-start(s8[7340032]{0:T(1024)(128)(4,1)} %bitcast.54), calls=%async_computation.7 | async-start | bytes 8388608
  481.9 9.3 %slice-start.1 = ((s8[7340032]{0:T(1024)(128)(4,1)}), s8[3145728]{0:T(1024)(128)(4,1)S(1)}, s32[]{:S(2)}) async-start(s8[7340032]{0:T(1024)(128)(4,1)} %bitcast.54), calls=%async_computation.8 | async-start | bytes 6291456
  481.9 9.3 %copy-start.2 = (bf16[256,3584]{1,0:T(8,128)(2,1)S(1)}, bf16[256,3584]{1,0:T(8,128)(2,1)}, u32[]{:S(2)}) copy-start(bf16[256,3584]{1,0:T(8,128)(2,1)} %reshape.323) | copy-start | bytes 5505028
  491.2 26.2 %copy-start.4 = (s32[16,8]{0,1:T(8,128)S(1)}, s32[16,8]{0,1:T(8,128)}, u32[]{:S(2)}) copy-start(s32[16,8]{0,1:T(8,128)} %param.13) | copy-start | bytes 1540
  508.2 77.7 %all-to-all-start.6 = ((bf16[128,2,1024]{2,1,0:T(2,128)(2,1)}), bf16[128,2,1024]{2,1,0:T(2,128)(2,1)S(1)}, u32[]{:S(2)}, u32[]{:S(2)}) async-start(bf16[128,2,1024]{2,1,0:T(2,128)(2,1)} %reshape.324), calls=%async_computation.6 | async-start | bytes 1048576 | tf_op jit(solution)/shard_map/all_to_all | solution.py:104
  587.1 7.0 %copy-start.1 = (bf16[16,3584]{1,0:T(8,128)(2,1)S(1)}, bf16[16,3584]{1,0:T(8,128)(2,1)}, u32[]{:S(2)}) copy-start(bf16[16,3584]{1,0:T(8,128)(2,1)} %param.10) | copy-start | bytes 344068
where the time goes:
time: 595 us; the launch traced here: 594 us
  waiting for transfers between devices  302 us (51%)
  blocking collectives  134 us (23%)
  local copies, waits for them, and re-layouts  63 us (11%)
  starting transfers between devices  45.2 us (8%)
  other arithmetic  31 us (5%)
  matrix products  17.4 us (3%)
    all_to_all x1, waiting for transfers between devices, per_device(): lax.all_to_all(split_values, 'dev', split_axis=1, concat_axis=1, tiled=True)  212 us
    unnamed x2, blocking collectives  134 us
    all_to_all x1, waiting for transfers between devices, per_device(): lax.all_to_all(send_values, 'dev', split_axis=0, concat_axis=0, tiled=True)  77.2 us
    convert_element_type x2, other arithmetic, dequantize(): return scaled.reshape(D, FF).astype(jnp.bfloat16)  27.9 us
    dot_general x1, matrix products, per_device(): jnp.dot(row_block.reshape(leading * item_count, width_in), joined, prefer...  15.5 us
    reshape x1, local copies, waits for them, and re-layouts, spread_parts(): values.reshape(holding, parts_count, width_in // parts_count, hidden)  13.7 us
    all_to_all x1, local copies, waits for them, and re-layouts, per_device(): lax.all_to_all(split_values, 'dev', split_axis=1, concat_axis=1, tiled=True)  13.7 us
  transfers between devices with their start and end apart: 7, of which 4 were waited for; matrix products, arithmetic and copies ran while one was open for 13% of the time, Pallas kernels for 0%

commit v1 on v0

--- a/solution.py
+++ b/solution.py
@@ -32,6 +32,16 @@
 
 
 def per_device(primary_q, primary_scales, new_place, tokens, experts, replica, route_num):
+
+    def choose_target_all(point):
+        response = jnp.concatenate(
+            jax.lax.all_to_all(
+                jnp.stack(jnp.split(point, jax.lax.axis_size("dev"), 1), 0), "dev", 0, 0
+            ),
+            1,
+        )
+        return response
+
     place_all = lax.all_gather(new_place, ("group", "dev"), axis=0, tiled=True)
     holding = primary_q.shape[0]
     parts_count = lax.axis_size("dev")
@@ -39,7 +49,7 @@
     wanted = lax.dynamic_slice_in_dim(place_all, first_dev, parts_count)
     split_values, split_scales = spread_parts(primary_q, primary_scales, parts_count)
     got_values, got_scales = (
-        lax.all_to_all(split_values, "dev", split_axis=1, concat_axis=1, tiled=True),
+        choose_target_all(split_values),
         lax.all_to_all(split_scales, "dev", split_axis=1, concat_axis=1, tiled=True),
     )
     send_values, send_scales = pick_parts(got_values, got_scales, wanted, first_dev)

time: 595 us -> 618 us (1.039)
  local copies, waits for them, and re-layouts: 63 us -> 84.2 us
    unnamed x22 -> x37, local copies, waits for them, and re-layouts: 10.3 us -> 43 us
    all_to_all x1 -> x0, local copies, waits for them, and re-layouts: 13.7 us -> none  [per_device(): lax.all_to_all(split_values, 'dev', split_axis=1, concat_axis=1, tiled=True)]
  transfers between devices with their start and end apart: 7 -> 7, of which waited for: 4 -> 5; matrix products, arithmetic and copies ran while one was open for 13% -> 16% of each run, Pallas kernels for 0% -> 0%
where the time goes in v1:
time: 618 us; the launch traced here: 617 us
  waiting for transfers between devices  303 us (49%)
  blocking collectives  134 us (22%)
  local copies, waits for them, and re-layouts  84.2 us (14%)
  starting transfers between devices  45.1 us (7%)
  other arithmetic  31 us (5%)
  matrix products  17.4 us (3%)
    all_to_all x1, waiting for transfers between devices, choose_target_all(): jax.lax.all_to_all(jnp.stack(jnp.split(point, jax.lax.axis_size('dev'), 1...  210 us
    unnamed x2, blocking collectives  134 us
    all_to_all x1, waiting for transfers between devices, per_device(): lax.all_to_all(send_values, 'dev', split_axis=0, concat_axis=0, tiled=True)  77.2 us
    unnamed x37, local copies, waits for them, and re-layouts  43 us
    convert_element_type x2, other arithmetic, dequantize(): return scaled.reshape(D, FF).astype(jnp.bfloat16)  27.9 us
    dot_general x1, matrix products, per_device(): jnp.dot(row_block.reshape(leading * item_count, width_in), joined, prefer...  15.5 us
    reshape x1, local copies, waits for them, and re-layouts, choose_target_all(): jnp.concatenate(jax.lax.all_to_all(jnp.stack(jnp.split(point, jax.lax.axi...  13.7 us
  transfers between devices with their start and end apart: 7, of which 5 were waited for; matrix products, arithmetic and copies ran while one was open for 16% of the time, Pallas kernels for 0%

profile of v1, /device:TPU:1, one launch (start us, length us, event | category | flops | bytes accessed | tf_op | source)
XLA Modules:
  0.0 616.9 jit_solution(696003792702877784)
XLA Ops:
  0.6 0.7 broadcast_bitcast_fusion
  1.4 0.7 reshape.356
  2.1 8.4 %all-to-all-start.2 = ((bf16[16,2,224]{2,1,0:T(2,128)(2,1)}), bf16[16,2,224]{2,1,0:T(2,128)(2,1)S(1)}, u32[]{:S(2)}, u32[]{:S(2)}) async-start(bf16[16,2,224]{2,1,0:T(2,128)(2,1)} %reshape.356), calls=%async_computation.2 | async-start | bytes 32768 | tf_op jit(solution)/shard_map/all_to_all | solution.py:53
  11.3 66.6 %all-reduce = s32[128]{0:T(128)S(1)} all-reduce(s32[128]{0:T(128)S(1)} %dynamic-update-slice), channel_id=1, replica_groups=mesh['group'=8,'dev'=16] {'group','dev'}, use_global_device_ids=true, to_apply=%add | all-reduce | flops 128 | bytes 1024
  77.9 0.8 copy.134
  78.7 0.2 compare_reduce_fusion.3
  78.9 0.2 fusion.33
  79.1 0.8 copy.133
  80.0 0.2 convert_reduce_fusion
  80.2 2.2 fusion.28
  82.4 2.2 fusion.27
  84.6 2.2 fusion.26
  86.7 2.2 fusion.25
  88.9 2.2 fusion.24
  91.1 2.2 fusion.23
  93.2 2.2 fusion.22
  95.4 2.2 fusion.21
  97.6 2.2 fusion.20
  99.8 2.2 fusion.19
  101.9 2.2 fusion.18
  104.1 2.3 fusion.17
  106.4 2.2 fusion.16
  108.6 2.2 fusion.15
  110.8 2.2 fusion.14
  113.0 0.1 select_reduce_fusion
  113.2 0.8 convert_element_type.161
  114.0 4.9 all-to-all-start.4
  119.0 1.2 gather_fusion.1
  120.2 8.4 %all-to-all-done.4 = bf16[128,1,2]{2,1,0:T(2,128)(2,1)S(1)} async-done(((bf16[128,1,2]{2,1,0:T(2,128)(2,1)}), bf16[128,1,2]{2,1,0:T(2,128)(2,1)S(1)}, u32[]{:S(2)}, u32[]{:S(2)}) %all-to-all-start.4) | async-done | bytes 544 | tf_op jit(solution)/shard_map/all_to_all | solution.py:91
  128.6 3.5 all-to-all-start.3
  132.1 2.2 fusion.13
  134.3 4.2 all-to-all-done.3
  138.5 5.0 all-to-all-start
  143.8 0.1 fusion.32
  144.0 0.7 convolution_convert_fusion
  144.6 1.7 reshape.322
  146.3 209.8 %all-to-all-done = bf16[16,2,1,224,1024]{4,3,1,2,0:T(8,128)(2,1)} async-done(((bf16[16,2,1,224,1024]{4,3,1,2,0:T(8,128)(2,1)}), bf16[16,2,1,224,1024]{4,3,1,2,0:T(8,128)(2,1)}, u32[]{:S(2)}, u32[]{:S(2)}) %all-to-all-start) | async-done | bytes 14680096 | tf_op jit(solution)/shard_map/all_to_all | solution.py:38
  356.1 9.3 %all-to-all-start.5 = ((bf16[128,2,3584]{2,1,0:T(2,128)(2,1)}), bf16[128,2,3584]{2,1,0:T(2,128)(2,1)S(1)}, u32[]{:S(2)}, u32[]{:S(2)}) async-start(bf16[128,2,3584]{2,1,0:T(2,128)(2,1)} %reshape.322), calls=%async_computation.5 | async-start | bytes 3670016 | tf_op jit(solution)/shard_map/all_to_all | solution.py:88
  365.4 13.7 %copy.131 = bf16[2,16,1,224,1024]{4,3,1,0,2:T(8,128)(2,1)} copy(bf16[2,16,1,224,1024]{4,3,0,2,1:T(8,128)(2,1)} %bitcast.17) | data formatting | bytes 29360128 | tf_op jit(solution)/shard_map/reshape | solution.py:37
  379.1 9.2 %gather_fusion = bf16[16,224,1024]{2,1,0:T(8,128)(2,1)} fusion(bf16[32,224,1024]{2,1,0:T(8,128)(2,1)} %bitcast.163, s32[1024]{0:T(1024)S(1)} %pad_clamp_fusion), kind=kCustom, calls=%fused_computation | custom fusion | bytes 14680128 | tf_op jit(solution)/shard_map/gather | solution.py:29
  388.4 3.9 all-to-all-done.5
  392.3 4.9 all-to-all-start.1
  397.4 1.0 mul.65
  398.4 6.2 %mul.68 = f32[28,128,8,128]{3,2,1,0:T(8,128)} broadcast(f32[28,8]{1,0:T(8,128)S(1)} %copy.141), dimensions={0,2} | broadcast | bytes 14680960 | tf_op jit(solution)/shard_map/mul | solution.py:14
  404.6 18.6 %fusion.8 = (bf16[3584,1024]{1,0:T(8,128)(2,1)}, bf16[3584,1024]{1,0:T(8,128)(2,1)}) fusion(f32[448,8,8,128]{3,2,1,0:T(8,128)S(1)} %bitcast.144, bf16[2,3584,1024]{2,1,0:T(8,128)(2,1)} %param.7, f32[448,8,8,128]{3,2,1,0:T(8,128)} %bitcast.145), kind=kLoop, calls=%fused_computation.13 | loop fusion | flops 22020096 | bytes 58720256 | tf_op jit(solution)/shard_map/convert_element_type | solution.py:15
  423.2 0.6 compare_reduce_fusion.2
  423.9 0.1 eq.167
  424.0 0.1 eq.164
  424.2 0.1 eq.158
  424.3 0.6 bitcast_convert_fusion
  425.0 1.7 reshape.323
  426.7 77.2 %all-to-all-done.1 = bf16[16,224,1024]{2,1,0:T(8,128)(2,1)} async-done(((bf16[16,224,1024]{2,1,0:T(8,128)(2,1)}), bf16[16,224,1024]{2,1,0:T(8,128)(2,1)}, u32[]{:S(2)}, u32[]{:S(2)}) %all-to-all-start.1) | async-done | bytes 7340064 | tf_op jit(solution)/shard_map/all_to_all | solution.py:57
  503.8 1.0 mul.71
  504.9 9.2 %fusion.6 = bf16[3584,1024]{1,0:T(8,128)(2,1)} fusion(f32[448,8,8,128]{3,2,1,0:T(8,128)S(1)} %bitcast.146, bf16[16,224,1024]{2,1,0:T(8,128)(2,1)} %all-to-all-done.1), kind=kLoop, calls=%fused_computation.9 | loop fusion | flops 11010048 | bytes 29360128 | tf_op jit(solution)/shard_map/convert_element_type | solution.py:15
  514.1 15.5 %fusion = f32[256,3072]{1,0:T(8,128)S(1)} fusion(bf16[256,3584]{1,0:T(8,128)(2,1)S(1)} %copy-done.2, bf16[3584,1024]{1,0:T(8,128)(2,1)} %fusion.6, bf16[3584,1024]{1,0:T(8,128)(2,1)} %get-tuple-element.12, bf16[3584,1024]{1,0:T(8,128)(2,1)S(1)} %bitcast.165), kind=kOutput, calls=%fused_computation.2 | convolution fusion | flops 5703204864 | bytes 27000832 | tf_op jit(solution)/shard_map/dot_general | solution.py:95
  529.7 0.5 multiply_convert_fusion
  530.1 1.0 reshape.324
  531.1 9.0 %all-to-all-start.6 = ((bf16[128,2,1024]{2,1,0:T(2,128)(2,1)}), bf16[128,2,1024]{2,1,0:T(2,128)(2,1)S(1)}, u32[]{:S(2)}, u32[]{:S(2)}) async-start(bf16[128,2,1024]{2,1,0:T(2,128)(2,1)} %reshape.324), calls=%async_computation.6 | async-start | bytes 1048576 | tf_op jit(solution)/shard_map/all_to_all | solution.py:114
  540.4 0.2 fusion.37
  540.6 67.6 %all-reduce.1 = f32[128,3]{1,0:T(8,128)S(1)} all-reduce(f32[128,3]{1,0:T(8,128)S(1)} %fusion.37), channel_id=2, replica_groups=mesh['group'=8,'dev'=16] {'group','dev'}, use_global_device_ids=true, to_apply=%region_5.6.clone | all-reduce | flops 384 | bytes 3072
  608.2 0.5 dynamic-slice_convert_fusion
  608.7 0.2 reshape.325
  608.9 1.0 fusion.10
  609.9 7.0 %copy.183 = bf16[1,3584,1024]{2,1,0:T(8,128)(2,1)} copy(bf16[1,3584,1024]{2,1,0:T(8,128)(2,1)} %bitcast.19) | data formatting | bytes 14680064
  (42 shorter events, 1.3 us)
Async XLA Ops:
  0.6 143.3 %copy-start = (bf16[16,3584]{1,0:T(8,128)(2,1)S(1)}, bf16[16,3584]{1,0:T(8,128)(2,1)}, u32[]{:S(2)}) copy-start(bf16[16,3584]{1,0:T(8,128)(2,1)} %param.10) | copy-start | bytes 344068
  2.1 111.9 %all-to-all-start.2 = ((bf16[16,2,224]{2,1,0:T(2,128)(2,1)}), bf16[16,2,224]{2,1,0:T(2,128)(2,1)S(1)}, u32[]{:S(2)}, u32[]{:S(2)}) async-start(bf16[16,2,224]{2,1,0:T(2,128)(2,1)} %reshape.356), calls=%async_computation.2 | async-start | bytes 32768 | tf_op jit(solution)/shard_map/all_to_all | solution.py:53
  114.0 14.6 %all-to-all-start.4 = ((bf16[128,1,2]{2,1,0:T(2,128)(2,1)}), bf16[128,1,2]{2,1,0:T(2,128)(2,1)S(1)}, u32[]{:S(2)}, u32[]{:S(2)}) async-start(bf16[128,1,2]{2,1,0:T(2,128)(2,1)} %convert_element_type.161), calls=%async_computation.4 | async-start | bytes 131072 | tf_op jit(solution)/shard_map/all_to_all | solution.py:91
  128.6 9.9 %all-to-all-start.3 = ((bf16[16,28,8]{1,2,0:T(8,128)(2,1)}), bf16[16,28,8]{1,2,0:T(8,128)(2,1)S(1)}, u32[]{:S(2)}, u32[]{:S(2)}) async-start(bf16[16,28,8]{1,2,0:T(8,128)(2,1)} %gather_fusion.1), calls=%async_computation.3 | async-start | bytes 65536 | tf_op jit(solution)/shard_map/all_to_all | solution.py:58
  138.5 217.6 %all-to-all-start = ((bf16[16,2,1,224,1024]{4,3,1,2,0:T(8,128)(2,1)}), bf16[16,2,1,224,1024]{4,3,1,2,0:T(8,128)(2,1)}, u32[]{:S(2)}, u32[]{:S(2)}) async-start(bf16[16,2,1,224,1024]{4,3,1,2,0:T(8,128)(2,1)} %fusion.13), calls=%async_computation | async-start | bytes 29360128 | tf_op jit(solution)/shard_map/all_to_all | solution.py:38
  356.1 36.2 %all-to-all-start.5 = ((bf16[128,2,3584]{2,1,0:T(2,128)(2,1)}), bf16[128,2,3584]{2,1,0:T(2,128)(2,1)S(1)}, u32[]{:S(2)}, u32[]{:S(2)}) async-start(bf16[128,2,3584]{2,1,0:T(2,128)(2,1)} %reshape.322), calls=%async_computation.5 | async-start | bytes 3670016 | tf_op jit(solution)/shard_map/all_to_all | solution.py:88
  379.1 18.0 %copy-start.3 = (bf16[2,28,8]{1,2,0:T(8,128)(2,1)S(1)}, bf16[2,28,8]{1,2,0:T(8,128)(2,1)}, u32[]{:S(2)}) copy-start(bf16[2,28,8]{1,2,0:T(8,128)(2,1)} %param.8) | copy-start | bytes 2692
  392.3 111.5 %all-to-all-start.1 = ((bf16[16,224,1024]{2,1,0:T(8,128)(2,1)}), bf16[16,224,1024]{2,1,0:T(8,128)(2,1)}, u32[]{:S(2)}, u32[]{:S(2)}) async-start(bf16[16,224,1024]{2,1,0:T(8,128)(2,1)} %gather_fusion), calls=%async_computation.1 | async-start | bytes 14680064 | tf_op jit(solution)/shard_map/all_to_all | solution.py:57
  503.8 10.3 %slice-start = ((s8[7340032]{0:T(1024)(128)(4,1)}), s8[4194304]{0:T(1024)(128)(4,1)S(1)}, s32[]{:S(2)}) async-start(s8[7340032]{0:T(1024)(128)(4,1)} %bitcast.164), calls=%async_computation.7 | async-start | bytes 8388608
  504.8 9.3 %slice-start.1 = ((s8[7340032]{0:T(1024)(128)(4,1)}), s8[3145728]{0:T(1024)(128)(4,1)S(1)}, s32[]{:S(2)}) async-start(s8[7340032]{0:T(1024)(128)(4,1)} %bitcast.164), calls=%async_computation.8 | async-start | bytes 6291456
  504.9 9.3 %copy-start.2 = (bf16[256,3584]{1,0:T(8,128)(2,1)S(1)}, bf16[256,3584]{1,0:T(8,128)(2,1)}, u32[]{:S(2)}) copy-start(bf16[256,3584]{1,0:T(8,128)(2,1)} %reshape.323) | copy-start | bytes 5505028
  514.1 26.1 %copy-start.4 = (s32[16,8]{0,1:T(8,128)S(1)}, s32[16,8]{0,1:T(8,128)}, u32[]{:S(2)}) copy-start(s32[16,8]{0,1:T(8,128)} %param.13) | copy-start | bytes 1540
  514.1 102.7 %copy-start.1 = (bf16[16,3584]{1,0:T(8,128)(2,1)S(1)}, bf16[16,3584]{1,0:T(8,128)(2,1)}, u32[]{:S(2)}) copy-start(bf16[16,3584]{1,0:T(8,128)(2,1)} %param.10) | copy-start | bytes 344068
  531.1 77.6 %all-to-all-start.6 = ((bf16[128,2,1024]{2,1,0:T(2,128)(2,1)}), bf16[128,2,1024]{2,1,0:T(2,128)(2,1)S(1)}, u32[]{:S(2)}, u32[]{:S(2)}) async-start(bf16[128,2,1024]{2,1,0:T(2,128)(2,1)} %reshape.324), calls=%async_computation.6 | async-start | bytes 1048576 | tf_op jit(solution)/shard_map/all_to_all | solution.py:114
